TPU v7x, 32 devices: a whole 2x2x4 slice. The times are simulated.
32 devices in a mesh: seq: 8 (over y, x, core), sub: 4 (over z).
Axes of the slice: x: 2, y: 2, z: 4, core: 2. Of those that a mesh axis runs over, the one named last changes fastest.
Arguments:
- query_rows: bfloat16 [8192, 1120], P(('seq', 'sub')), may hold values from -6 to 6
- key_rows: bfloat16 [8192, 1120], P(('seq', 'sub')), may hold values from -6 to 6
- value_rows: bfloat16 [8192, 1120], P(('seq', 'sub')), may hold values from -6 to 6
- query_tangent: bfloat16 [8192, 1120], P(('seq', 'sub')), may hold values from -6 to 6
- key_tangent: bfloat16 [8192, 1120], P(('seq', 'sub')), may hold values from -6 to 6
- value_tangent: bfloat16 [8192, 1120], P(('seq', 'sub')), may hold values from -6 to 6
- teacher: bfloat16 [8192, 2240], P(('seq', 'sub')), may hold values from -64 to 64
- out_weight: bfloat16 [1120, 2240], replicated, may hold values from -0.1875 to 0.1875
- norm_gain: float32 [1120], replicated, may hold values from 0.1 to 1.9
- clip_length: int32 [1], replicated, may hold values from 4096 to 8192
- block_mask: int32 [128], P(('seq', 'sub')), may hold values 0 or 1
Outputs:
- residual: bfloat16 [8192, 2240], P(('seq', 'sub'))
- grad_query: bfloat16 [8192, 1120], P(('seq', 'sub'))
- grad_key: bfloat16 [8192, 1120], P(('seq', 'sub'))
- grad_value: bfloat16 [8192, 1120], P(('seq', 'sub'))
All inputs are finite; a program needn't handle non-finite values. No bound on the sum of `block_mask` on one device may be relied on, other than what follows from the above.
Results may differ from a plain program's by a relative error of at most 0.007.
Values may be sent and summed in bfloat16 or wider, within the bound.
A program may use at most 64 MiB of HBM per device.

v0:
```python
import jax
import jax.numpy as jnp
from jax import lax
from jax.sharding import PartitionSpec as P

H = 10
E = 112
BLK = 64


def split_heads(matrix):
    return matrix.reshape(matrix.shape[0], H, E)


def norm_back(unnorm, scale_inv, weighted):
    inner_mean = jnp.mean(unnorm * weighted, axis=-1, keepdims=True)
    return scale_inv * weighted - unnorm * (scale_inv * scale_inv * scale_inv) * inner_mean


def combine_states(stacked):
    totals = lax.psum(stacked, ("seq", "sub"))
    return totals.astype(jnp.bfloat16)


def local(
    query_rows,
    key_rows,
    value_rows,
    query_tangent,
    key_tangent,
    value_tangent,
    teacher,
    out_weight,
    norm_gain,
    clip_length,
    block_mask,
):
    f32 = jnp.float32
    bf16 = jnp.bfloat16
    tok_rows = query_rows.shape[0]
    first_row = (lax.axis_index("seq") * lax.axis_size("sub") + lax.axis_index("sub")) * tok_rows
    position = first_row + lax.iota(jnp.int32, tok_rows)
    block_flags = jnp.broadcast_to(block_mask[:, None], (tok_rows // BLK, BLK)).reshape(tok_rows)
    valid_rows = jnp.where((position < clip_length[0]) & (block_flags == 1), 1.0, 0.0).astype(f32)[
        :, None
    ]
    key_vals = key_rows.astype(f32)
    key_feat = (valid_rows * jnp.maximum(key_vals, 0.0)).astype(bf16)
    key_slope = valid_rows * jnp.where(key_vals > 0, 1.0, 0.0).astype(f32)
    key_dot = (key_slope * key_tangent.astype(f32)).astype(bf16)
    value_heads = split_heads(value_rows)
    feat_keys = split_heads(key_feat)
    state_part = jnp.einsum("the,thf->hef", feat_keys, value_heads, preferred_element_type=f32)
    tangent_part = jnp.einsum(
        "the,thf->hef", split_heads(key_dot), value_heads, preferred_element_type=f32
    ) + jnp.einsum(
        "the,thf->hef", feat_keys, split_heads(value_tangent), preferred_element_type=f32
    )
    states = combine_states(jnp.stack([state_part, tangent_part]))
    state = states[0]
    state_dot = states[1]
    query_vals = query_rows.astype(f32)
    query_feat = jnp.maximum(query_vals, 0.0).astype(bf16)
    query_slope = jnp.where(query_vals > 0, 1.0, 0.0).astype(f32)
    query_dot = (query_slope * query_tangent.astype(f32)).astype(bf16)
    feat_heads = split_heads(query_feat)
    unnorm = jnp.einsum("the,hef->thf", feat_heads, state, preferred_element_type=f32)
    unnorm_dot = jnp.einsum(
        "the,hef->thf", split_heads(query_dot), state, preferred_element_type=f32
    ) + jnp.einsum("the,hef->thf", feat_heads, state_dot, preferred_element_type=f32)
    gain_heads = norm_gain.reshape(H, E)
    scale_inv = lax.rsqrt(jnp.mean(unnorm * unnorm, axis=-1, keepdims=True) + 1e-06)
    normed_dot = (
        (gain_heads * norm_back(unnorm, scale_inv, unnorm_dot))
        .astype(bf16)
        .reshape(tok_rows, H * E)
    )
    velocity = jnp.dot(normed_dot, out_weight, preferred_element_type=f32)
    residual = (velocity - teacher.astype(f32)).astype(bf16)
    normed_grad = lax.dot_general(
        residual, out_weight, (((1,), (1,)), ((), ())), preferred_element_type=f32
    )
    unnorm_grad = norm_back(unnorm, scale_inv, gain_heads * split_heads(normed_grad)).astype(bf16)
    grad_part = jnp.einsum("the,thf->hef", feat_heads, unnorm_grad, preferred_element_type=f32)
    state_grad = combine_states(grad_part[None])[0]
    grad_query = (
        query_slope
        * jnp.einsum("thf,hef->the", unnorm_grad, state, preferred_element_type=f32).reshape(
            tok_rows, H * E
        )
    ).astype(bf16)
    grad_key = (
        key_slope
        * jnp.einsum("thf,hef->the", value_heads, state_grad, preferred_element_type=f32).reshape(
            tok_rows, H * E
        )
    ).astype(bf16)
    grad_value = (
        jnp.einsum("the,hef->thf", feat_keys, state_grad, preferred_element_type=f32)
        .reshape(tok_rows, H * E)
        .astype(bf16)
    )
    return (residual, grad_query, grad_key, grad_value)


def solution(mesh):
    return jax.shard_map(
        local,
        mesh=mesh,
        in_specs=(
            P(("seq", "sub"), None),
            P(("seq", "sub"), None),
            P(("seq", "sub"), None),
            P(("seq", "sub"), None),
            P(("seq", "sub"), None),
            P(("seq", "sub"), None),
            P(("seq", "sub"), None),
            P(),
            P(),
            P(),
            P(("seq", "sub")),
        ),
        out_specs=(
            P(("seq", "sub"), None),
            P(("seq", "sub"), None),
            P(("seq", "sub"), None),
            P(("seq", "sub"), None),
        ),
        check_vma=False,
    )
```

profile of v0, /device:TPU:0, one launch (start us, length us, event | category | flops | bytes accessed | tf_op | source)
XLA Modules:
  0.0 119.9 jit_solution(6810560053801250112)
XLA Ops:
  0.6 0.0 copy-start
  1.4 0.4 copy-done
  1.7 0.7 broadcast_compare_fusion
  2.4 0.1 broadcast_in_dim.29
  2.4 0.1 eq.16
  2.5 0.8 mul.117
  3.3 1.6 %fusion.4 = (bf16[256,1120]{0,1:T(8,128)(2,1)S(1)}, bf16[256,1120]{0,1:T(8,128)(2,1)S(1)}) fusion(bf16[256,1120]{0,1:T(8,128)(2,1)} %param.12, f32[256]{0:T(256)S(1)} %and_select_fusion, bf16[256,1120]{0,1:T(8,128)(2,1)} %param.15), kind=kLoop, calls=%fused_computation.17 | loop fusion | flops 2867200 | bytes 2294784 | tf_op jit(solution)/shard_map/convert_element_type | solution.py:48
  4.9 0.0 copy-start.3
  5.0 0.3 fusion.16
  5.3 0.7 copy-done.3
  6.0 0.3 fusion.2
  6.3 0.3 convolution_bitcast_fusion.2
  6.6 0.1 pad_maximum_fusion
  6.7 0.0 copy-start.1
  6.7 53.7 %all-reduce.2 = bf16[2,10,112,112]{3,2,1,0:T(8,128)(2,1)S(1)} all-reduce(f32[2,10,112,112]{3,2,1,0:T(8,128)S(1)} %pad_maximum_fusion), channel_id=1, replica_groups=mesh['seq'=8,'sub'=4] {'seq','sub'}, use_global_device_ids=true, to_apply=%region_0.1 | all-reduce | flops 250880 | bytes 1505280 | tf_op jit(solution)/shard_map/psum | solution.py:21
  60.4 0.0 copy-done.1
  60.5 0.0 slice-start
  60.5 1.5 %fusion.5 = (bf16[256,1120]{0,1:T(8,128)(2,1)S(1)}, bf16[256,1120]{0,1:T(8,128)(2,1)S(1)}) fusion(bf16[256,1120]{0,1:T(8,128)(2,1)S(1)} %copy-done.1, bf16[256,1120]{0,1:T(8,128)(2,1)} %param.14), kind=kLoop, calls=%fused_computation.18 | loop fusion | flops 2293760 | bytes 2293760 | tf_op jit(solution)/shard_map/convert_element_type | solution.py:63
  61.9 0.4 fusion.13
  62.3 0.0 slice-start.1
  62.3 0.4 fusion.1
  62.7 0.4 multiply_reduce_fusion.2
  63.1 0.0 copy-start.4
  63.1 0.6 multiply_convert_fusion
  63.7 0.0 slice-done
  63.7 0.0 slice-done.1
  63.7 0.7 copy-done.4
  64.5 2.3 %fusion = bf16[256,2240]{0,1:T(8,128)(2,1)S(1)} fusion(bf16[256,1120]{0,1:T(8,128)(2,1)S(1)} %bitcast.81, bf16[1120,2240]{1,0:T(8,128)(2,1)S(1)} %bitcast.83, bf16[256,2240]{0,1:T(8,128)(2,1)S(1)} %copy-done.4), kind=kOutput, calls=%fused_computation.1 | convolution fusion | flops 1286225920 | bytes 7884800 | tf_op jit(solution)/shard_map/dot_general | solution.py:78
  66.8 0.0 copy-start.5
  66.8 1.5 %fusion.17 = f32[256,1120]{0,1:T(8,128)S(1)} fusion(bf16[1120,2240]{1,0:T(8,128)(2,1)S(1)} %bitcast.83, bf16[256,2240]{0,1:T(8,128)(2,1)S(1)} %fusion), kind=kOutput, calls=%fused_computation.47 | convolution fusion | flops 1284505600 | bytes 7311360 | tf_op jit(solution)/shard_map/dot_general | solution.py:80
  68.3 0.0 copy-done.5
  68.3 0.2 multiply_reduce_fusion
  68.6 0.3 subtract_convert_fusion
  68.9 0.3 convolution_bitcast_fusion.1
  69.2 0.3 fusion.12
  69.5 1.0 fusion.7
  70.5 46.1 %all-reduce.3 = bf16[1,10,112,112]{3,2,1,0:T(8,128)(2,1)S(1)} all-reduce(f32[1,10,112,112]{3,2,1,0:T(8,128)S(1)} %convolution_bitcast_fusion.1), channel_id=1, replica_groups=mesh['seq'=8,'sub'=4] {'seq','sub'}, use_global_device_ids=true, to_apply=%region_4.5 | all-reduce | flops 125440 | bytes 752640 | tf_op jit(solution)/shard_map/psum | solution.py:21
  116.6 1.2 convolution_convert_fusion
  117.8 0.0 copy-start.2
  117.8 0.3 fusion.10
  118.1 0.8 copy-done.2
  118.9 1.0 fusion.8
  (4 shorter events, 0.0 us)
Async XLA Ops:
  0.6 1.1 copy-start
  4.9 1.1 copy-start.3
  6.7 53.7 %copy-start.1 = (bf16[256,1120]{0,1:T(8,128)(2,1)S(1)}, bf16[256,1120]{0,1:T(8,128)(2,1)}, u32[]{:S(2)}) copy-start(bf16[256,1120]{0,1:T(8,128)(2,1)} %param.11) | copy-start | bytes 1720324
  60.5 3.3 %slice-start = ((s8[5160960]{0:T(1024)(128)(4,1)}), s8[4194304]{0:T(1024)(128)(4,1)S(1)}, s32[]{:S(2)}) async-start(s8[5160960]{0:T(1024)(128)(4,1)} %bitcast.82), calls=%async_computation | async-start | bytes 8388608
  62.3 1.4 %slice-start.1 = ((s8[5160960]{0:T(1024)(128)(4,1)}), s8[966656]{0:T(1024)(128)(4,1)S(1)}, s32[]{:S(2)}) async-start(s8[5160960]{0:T(1024)(128)(4,1)} %bitcast.82), calls=%async_computation.1 | async-start | bytes 1933312
  63.1 1.3 %copy-start.4 = (bf16[256,2240]{0,1:T(8,128)(2,1)S(1)}, bf16[256,2240]{0,1:T(8,128)(2,1)}, u32[]{:S(2)}) copy-start(bf16[256,2240]{0,1:T(8,128)(2,1)} %param.17) | copy-start | bytes 3440644
  66.8 1.5 %copy-start.5 = (bf16[256,2240]{0,1:T(8,128)(2,1)}, bf16[256,2240]{0,1:T(8,128)(2,1)S(1)}, u32[]{:S(2)}) copy-start(bf16[256,2240]{0,1:T(8,128)(2,1)S(1)} %fusion) | copy-start | bytes 3440644
  117.8 1.1 copy-start.2
where the time goes:
time: 120 us
  blocking collectives  99.8 us (83%)
  matrix products  7.92 us (7%)
  other arithmetic  7.01 us (6%)
  local copies, waits for them, and re-layouts  3.56 us (3%)
  between operations  1.56 us (1%)
    psum x2, blocking collectives, combine_states(): totals = lax.psum(stacked, ('seq', 'sub'))  99.8 us
    unnamed x16, local copies, waits for them, and re-layouts  2.62 us

commit v1 on v0

--- a/solution.py
+++ b/solution.py
@@ -2,6 +2,7 @@
 import jax.numpy as jnp
 from jax import lax
 from jax.sharding import PartitionSpec as P
+from jax.lax import psum
 
 H = 10
 E = 112
@@ -18,7 +19,8 @@
 
 
 def combine_states(stacked):
-    totals = lax.psum(stacked, ("seq", "sub"))
+    newest = psum(stacked, axis_name="seq")
+    totals = psum(newest, axis_name="sub")
     return totals.astype(jnp.bfloat16)
 
 

time: 120 us -> 226 us (1.88)
  waiting for transfers between devices: 0 us -> 109 us
  blocking collectives: 99.8 us -> 77.7 us
  between operations: 1.56 us -> 15 us
  matrix products: 7.92 us -> 12.5 us
    psum x0 -> x2, waiting for transfers between devices: none -> 109 us  [combine_states(): newest = psum(stacked, axis_name='seq')]
    psum x2, blocking collectives: 99.8 us -> 77.7 us  [combine_states(): totals = psum(newest, axis_name='sub')]
    dot_general x1, matrix products: 2.33 us -> 5.08 us  [local(): velocity = jnp.dot(normed_dot, out_weight, preferred_element_type=f32)]
  transfers between devices with their start and end apart: 0 -> 2, of which waited for: 0 -> 2; matrix products, arithmetic and copies ran while one was open for 0% -> 1% of each run, Pallas kernels for 0% -> 0%
where the time goes in v1:
time: 226 us
  waiting for transfers between devices  109 us (48%)
  blocking collectives  77.7 us (34%)
  between operations  15 us (7%)
  matrix products  12.5 us (6%)
  other arithmetic  8.03 us (4%)
  local copies, waits for them, and re-layouts  3.14 us (1%)
    psum x2, waiting for transfers between devices, combine_states(): newest = psum(stacked, axis_name='seq')  109 us
    psum x2, blocking collectives, combine_states(): totals = psum(newest, axis_name='sub')  77.7 us
    dot_general x1, matrix products, local(): velocity = jnp.dot(normed_dot, out_weight, preferred_element_type=f32)  5.08 us
  transfers between devices with their start and end apart: 2, of which 2 were waited for; matrix products, arithmetic and copies ran while one was open for 1% of the time, Pallas kernels for 0%

profile of v1, /device:TPU:0, one launch (start us, length us, event | category | flops | bytes accessed | tf_op | source)
XLA Modules:
  0.0 225.7 jit_solution(6961558122113905233)
XLA Ops:
  7.2 0.0 copy-start
  7.2 0.0 all-reduce.5.cloned.1.call-start
  7.9 0.7 broadcast_compare_fusion
  8.6 0.1 broadcast_in_dim.29
  8.7 0.1 eq.16
  8.8 1.6 fusion.4
  10.4 0.0 copy-done
  10.4 0.3 fusion.16
  10.7 0.0 copy-start.3
  10.7 0.3 convolution_bitcast_fusion.2
  11.0 0.7 copy-done.3
  11.8 0.3 fusion.2
  12.1 0.0 copy-start.5
  12.1 1.1 pad_maximum_fusion
  13.2 0.0 all-reduce.5.cloned.1.call-update
  13.2 0.0 all-reduce.7.cloned.1.call-start
  13.2 0.0 copy-done.5
  13.3 0.1 mul.117
  13.3 0.9 copy-done.1
  14.2 0.2 copy-done.4
  14.4 0.3 fusion.5
  14.7 58.5 %all-reduce.5.cloned.1.call-done = f32[2,10,112,112]{3,2,1,0:T(8,128)} async-done(((f32[2,10,112,112]{3,2,1,0:T(8,128)}), f32[2,10,112,112]{3,2,1,0:T(8,128)}) %all-reduce.5.cloned.1.call-update) | async-done | bytes 1003536 | tf_op jit(solution)/shard_map/psum | solution.py:22
  73.2 46.1 %all-reduce.8 = bf16[2,10,112,112]{3,2,1,0:T(8,128)(2,1)S(1)} all-reduce(f32[2,10,112,112]{3,2,1,0:T(8,128)} %all-reduce.5.cloned.1.call-done), channel_id=1, replica_groups=mesh['seq'=8,'sub'=4] {'sub'}, use_global_device_ids=true, to_apply=%region_1.2 | all-reduce | flops 250880 | bytes 1505280 | tf_op jit(solution)/shard_map/psum | solution.py:23
  119.3 0.4 fusion.13
  119.7 0.4 fusion.1
  120.1 0.0 copy-start.6
  120.1 0.4 multiply_reduce_fusion.2
  120.5 0.0 slice-start
  120.5 0.5 multiply_convert_fusion
  121.0 0.3 copy-done.6
  121.3 5.1 %fusion = bf16[256,2240]{0,1:T(8,128)(2,1)S(1)} fusion(bf16[256,1120]{0,1:T(8,128)(2,1)S(1)} %bitcast.81, bf16[1120,2240]{1,0:T(8,128)(2,1)} %param.18, bf16[256,2240]{0,1:T(8,128)(2,1)S(1)} %copy-done.6), kind=kOutput, calls=%fused_computation.1 | convolution fusion | flops 1286225920 | bytes 7884800 | tf_op jit(solution)/shard_map/dot_general | solution.py:80
  126.4 0.0 slice-done
  126.4 0.0 slice-done.1
  126.4 0.0 copy-start.7
  126.5 1.5 fusion.17
  128.0 0.0 copy-done.7
  128.0 0.2 multiply_reduce_fusion
  128.2 0.3 subtract_convert_fusion
  128.5 1.1 convolution_bitcast_fusion.1
  129.6 1.3 fusion.12
  130.9 0.0 all-reduce.7.cloned.1.call-update
  131.0 2.3 %fusion.7 = bf16[256,1120]{0,1:T(8,128)(2,1)} fusion(f32[10,112,256]{2,1,0:T(8,128)} %fusion.12, bf16[256,1120]{0,1:T(8,128)(2,1)S(1)} %copy-done.1), kind=kLoop, calls=%fused_computation.20 | loop fusion | flops 1433600 | bytes 2293760 | tf_op jit(solution)/shard_map/convert_element_type | solution.py:93
  133.2 50.8 %all-reduce.7.cloned.1.call-done = f32[1,10,112,112]{3,2,1,0:T(8,128)} async-done(((f32[1,10,112,112]{3,2,1,0:T(8,128)}), f32[1,10,112,112]{3,2,1,0:T(8,128)}) %all-reduce.7.cloned.1.call-update) | async-done | bytes 501776 | tf_op jit(solution)/shard_map/psum | solution.py:22
  184.0 31.6 %all-reduce.9 = bf16[1,10,112,112]{3,2,1,0:T(8,128)(2,1)S(1)} all-reduce(f32[1,10,112,112]{3,2,1,0:T(8,128)} %all-reduce.7.cloned.1.call-done), channel_id=1, replica_groups=mesh['seq'=8,'sub'=4] {'sub'}, use_global_device_ids=true, to_apply=%region_6.7 | all-reduce | flops 125440 | bytes 752640 | tf_op jit(solution)/shard_map/psum | solution.py:23
  215.6 1.2 convolution_convert_fusion
  216.8 0.3 fusion.10
  217.1 0.8 copy-done.2
  217.8 1.0 fusion.8
  (8 shorter events, 0.0 us)
Async XLA Ops:
  7.2 3.2 %copy-start = (bf16[256,1120]{0,1:T(8,128)(2,1)S(1)}, bf16[256,1120]{0,1:T(8,128)(2,1)}, u32[]{:S(2)}) copy-start(bf16[256,1120]{0,1:T(8,128)(2,1)} %param.13) | copy-start | bytes 1720324
  7.2 66.0 %all-reduce.5.cloned.1.call-start = ((), (), s32[]{:S(2)}) async-start(), calls=%async_computation | async-start | bytes 2293760 | tf_op jit(solution)/shard_map/psum | solution.py:22
  10.7 1.1 copy-start.3
  12.1 1.2 copy-start.5
  13.2 1.1 copy-start.1
  13.2 1.2 copy-start.4
  13.2 170.8 %all-reduce.7.cloned.1.call-start = ((), (), s32[]{:S(2)}) async-start(), calls=%async_computation.1 | async-start | bytes 1146880 | tf_op jit(solution)/shard_map/psum | solution.py:22
  120.1 1.3 copy-start.6
  120.5 5.9 %slice-start = ((s8[5160960]{0:T(1024)(128)(4,1)}), s8[4194304]{0:T(1024)(128)(4,1)S(1)}, s32[]{:S(2)}) async-start(s8[5160960]{0:T(1024)(128)(4,1)} %bitcast.82), calls=%async_computation.2 | async-start | bytes 8388608
  121.3 5.1 %slice-start.1 = ((s8[5160960]{0:T(1024)(128)(4,1)}), s8[966656]{0:T(1024)(128)(4,1)S(1)}, s32[]{:S(2)}) async-start(s8[5160960]{0:T(1024)(128)(4,1)} %bitcast.82), calls=%async_computation.3 | async-start | bytes 1933312
  126.4 1.5 copy-start.7
  216.8 1.1 copy-start.2
Sparse Core Ops, SparseCore 0:
  13.3 59.8 all-reduce.4
  131.1 52.8 all-reduce.6
